TPU v7x, 512 devices: a whole 4x4x16 slice. The times are simulated.
512 devices in a mesh: slab: 16 (over z_lo, core), src: 32 (over y, x, z_hi).
Axes of the slice: x: 4, y: 4, z: 16 (z_hi: 2, z_lo: 8; z = z_hi * 8 + z_lo), core: 2. Of those that a mesh axis runs over, the one named last changes fastest.
Arguments:
- trace_values: bfloat16 [32, 8192, 128], P('src', 'slab'), may hold values from -6 to 6
- trace_owner: int32 [32, 8192, 1], P('src', 'slab'), may hold values from 0 to 15; in each aligned block of 512 rows (0 to 511, 512 to 1023, ..., all dimensions but the last counted through in order) at most 64 rows name the same one
- trace_source: int32 [32, 8192], P('src', 'slab'), may hold values from 0 to 511
- source_fields: bfloat16 [2, 8192, 16384], P(None, 'slab', 'src'), may hold values from -0.03125 to 0.03125
- green_fields: bfloat16 [2, 2048, 16384], P(None, 'slab', 'src'), may hold values from -0.0625 to 0.0625
Outputs:
- gradient: float32 [16384], P('src')
Inputs may be any that keep to these rules, and one draw needn't show every extreme that they name: `trace_owner`: among the traces of one device, no owner is named by more than 64 traces, a bound that some block reaches.
All inputs are finite; a program needn't handle non-finite values.
Results may differ from a plain program's by a relative error of at most 0.0026.
Values may be sent and summed in bfloat16 or wider, within the bound.
A program may use at most 64 MiB of HBM per device.

v0:
```python
import jax
import jax.numpy as jnp
from jax import lax
from jax.sharding import PartitionSpec as P


def on_device(trace_values, trace_owner, trace_source, source_fields, green_fields):
    values = trace_values[0]
    owners = trace_owner[0, :, 0]
    locals_id = trace_source[0]
    trace_count = values.shape[0]
    width = values.shape[1]
    half_width = width // 2
    slab_count = lax.axis_size("slab")
    src_count = lax.axis_size("src")
    sources_here = source_fields.shape[1]
    source_ids = jnp.arange(sources_here, dtype=jnp.int32)
    iota_high = (source_ids // 32).astype(jnp.bfloat16)
    iota_low = (source_ids % 32).astype(jnp.bfloat16)
    capacity = 2 * trace_count // slab_count
    owner_hits = (owners[:, None] == jnp.arange(slab_count, dtype=jnp.int32)[None, :]).astype(
        jnp.int32
    )
    ranks = jnp.sum(jnp.cumsum(owner_hits, axis=0) * owner_hits, axis=1) - 1
    slots = owners * capacity + ranks
    placing = (
        jnp.arange(slab_count * capacity, dtype=jnp.int32)[:, None] == slots[None, :]
    ).astype(jnp.bfloat16)
    sent_values = jnp.dot(placing, values, preferred_element_type=jnp.float32).astype(jnp.bfloat16)
    labels = jnp.stack([locals_id // 32 + 1, locals_id % 32 + 1], axis=1).astype(jnp.bfloat16)
    sent_labels = (jnp.dot(placing, labels, preferred_element_type=jnp.float32) - 1.0).astype(
        jnp.bfloat16
    )
    got_values, got_labels = (
        lax.all_to_all(
            sent_values.reshape(slab_count, capacity, width),
            "slab",
            split_axis=0,
            concat_axis=0,
            tiled=True,
        ),
        lax.all_to_all(
            sent_labels.reshape(slab_count, capacity, 2),
            "slab",
            split_axis=0,
            concat_axis=0,
            tiled=True,
        ),
    )
    flat_labels = got_labels.reshape(-1, 2)
    picks = (
        (iota_high[:, None] == flat_labels[None, :, 0])
        & (iota_low[:, None] == flat_labels[None, :, 1])
    ).astype(jnp.bfloat16)
    assembled = jnp.dot(picks, got_values.reshape(-1, width), preferred_element_type=jnp.float32)
    residual_piece = assembled.astype(jnp.bfloat16)
    residual_rows = lax.all_gather(residual_piece, "src", axis=1, tiled=True)
    split_rows = residual_rows.reshape(sources_here, src_count, 2, half_width)
    res_real = split_rows[:, :, 0, :].reshape(sources_here, src_count * half_width)
    res_imag = split_rows[:, :, 1, :].reshape(sources_here, src_count * half_width)
    piece = lax.all_gather(green_fields, "slab", axis=1, tiled=True)
    adj_real = jnp.dot(res_real, piece[0], preferred_element_type=jnp.float32) + jnp.dot(
        res_imag, piece[1], preferred_element_type=jnp.float32
    )
    adj_imag = jnp.dot(res_real, piece[1], preferred_element_type=jnp.float32) - jnp.dot(
        res_imag, piece[0], preferred_element_type=jnp.float32
    )
    adj_real, adj_imag = (adj_real, adj_imag)
    partial_value = jnp.sum(
        source_fields[0].astype(jnp.float32) * adj_real
        - source_fields[1].astype(jnp.float32) * adj_imag,
        axis=0,
    )
    return lax.psum(partial_value, "slab")


def solution(mesh):
    in_specs = (
        P("src", "slab", None),
        P("src", "slab", None),
        P("src", "slab"),
        P(None, "slab", "src"),
        P(None, "slab", "src"),
    )
    out_specs = P("src")
    return jax.shard_map(
        on_device, mesh=mesh, in_specs=in_specs, out_specs=out_specs, check_vma=False
    )
```

profile of v0, /device:TPU:6, one launch (start us, length us, event | category | flops | bytes accessed | tf_op | source)
XLA Modules:
  0.0 432.0 jit_solution(941762704033851159)
XLA Ops:
  6.5 0.7 fusion.31
  7.3 1.1 reduce-window.6
  8.4 0.2 slice_reduce_fusion
  8.7 0.8 fusion.30
  9.4 0.7 add_add_fusion
  10.1 0.7 add_convert_fusion
  10.8 0.5 fusion.21
  11.4 0.6 copy.12
  12.0 12.6 %all-to-all-start = ((bf16[16,64,2]{1,2,0:T(2,128)(2,1)}), bf16[16,64,2]{1,2,0:T(2,128)(2,1)S(1)}, u32[]{:S(2)}, u32[]{:S(2)}) async-start(bf16[16,64,2]{1,2,0:T(2,128)(2,1)} %copy.12), calls=%async_computation | async-start | bytes 16384 | tf_op jit(solution)/shard_map/all_to_all | solution.py:42
  24.6 1.2 fusion.16
  25.8 9.2 %all-to-all-done = bf16[16,64,2]{1,2,0:T(2,128)(2,1)S(1)} async-done(((bf16[16,64,2]{1,2,0:T(2,128)(2,1)}), bf16[16,64,2]{1,2,0:T(2,128)(2,1)S(1)}, u32[]{:S(2)}, u32[]{:S(2)}) %all-to-all-start) | async-done | bytes 4128 | tf_op jit(solution)/shard_map/all_to_all | solution.py:42
  35.0 3.5 all-to-all-start.1
  38.7 14.7 %all-to-all-done.1 = bf16[16,64,128]{2,1,0:T(8,128)(2,1)S(1)} async-done(((bf16[16,64,128]{2,1,0:T(8,128)(2,1)}), bf16[16,64,128]{2,1,0:T(8,128)(2,1)S(1)}, u32[]{:S(2)}, u32[]{:S(2)}) %all-to-all-start.1) | async-done | bytes 262176 | tf_op jit(solution)/shard_map/all_to_all | solution.py:35
  53.4 1.3 fusion.17
  54.8 0.7 all-gather.5.cloned.1.call-update
  55.5 208.7 %all-gather.3.cloned.1.call-done = bf16[512,4096]{1,0:T(8,128)(2,1)} async-done(((bf16[512,128]{1,0:T(8,128)(2,1)}), bf16[512,4096]{1,0:T(8,128)(2,1)}) %all-gather.3.cloned.1.call-update) | async-done | bytes 4194320 | tf_op jit(solution)/shard_map/all_gather | solution.py:57
  264.2 6.5 %copy.14 = bf16[512,4096]{0,1:T(8,128)(2,1)} copy(bf16[512,4096]{1,0:T(8,128)(2,1)} %all-gather.3.cloned.1.call-done) | data formatting | bytes 8388608 | tf_op jit(solution)/shard_map/all_gather | solution.py:57
  270.7 4.0 fusion.47
  274.7 89.8 %all-gather.5.cloned.1.call-done = bf16[2,2048,512]{2,1,0:T(8,128)(2,1)} async-done(((bf16[2,128,512]{2,1,0:T(8,128)(2,1)}), bf16[2,2048,512]{2,1,0:T(8,128)(2,1)}) %all-gather.5.cloned.1.call-update) | async-done | bytes 4194320 | tf_op jit(solution)/shard_map/all_gather | solution.py:61
  364.5 3.0 fusion.7
  367.5 3.0 fusion.6
  370.6 1.3 fusion.11
  371.9 1.3 fusion.15
  373.2 51.9 %psum.7 = f32[512]{0:T(512)} all-reduce(f32[512]{0:T(512)S(1)} %fusion.15), channel_id=1, replica_groups=mesh['slab'=16,'src'=32] {'slab'}, use_global_device_ids=true, to_apply=%region_4.5 | all-reduce | flops 512 | bytes 4096 | tf_op jit(solution)/shard_map/psum | solution.py:74
  (19 shorter events, 0.4 us)
Async XLA Ops:
  6.5 18.1 %copy-start = (bf16[1,512,128]{2,1,0:T(8,128)(2,1)S(1)}, bf16[1,512,128]{2,1,0:T(8,128)(2,1)}, u32[]{:S(2)}) copy-start(bf16[1,512,128]{2,1,0:T(8,128)(2,1)} %param.5) | copy-start | bytes 393220
  12.0 23.0 %all-to-all-start = ((bf16[16,64,2]{1,2,0:T(2,128)(2,1)}), bf16[16,64,2]{1,2,0:T(2,128)(2,1)S(1)}, u32[]{:S(2)}, u32[]{:S(2)}) async-start(bf16[16,64,2]{1,2,0:T(2,128)(2,1)} %copy.12), calls=%async_computation | async-start | bytes 16384 | tf_op jit(solution)/shard_map/all_to_all | solution.py:42
  35.0 18.5 %all-to-all-start.1 = ((bf16[16,64,128]{2,1,0:T(8,128)(2,1)}), bf16[16,64,128]{2,1,0:T(8,128)(2,1)S(1)}, u32[]{:S(2)}, u32[]{:S(2)}) async-start(bf16[16,64,128]{2,1,0:T(8,128)(2,1)} %bitcast.6), calls=%async_computation.1 | async-start | bytes 524288 | tf_op jit(solution)/shard_map/all_to_all | solution.py:35
  38.5 225.7 %all-gather.3.cloned.1.call-start = ((), (), s32[]{:S(2)}) async-start(), calls=%async_computation.2 | async-start | bytes 4325376 | tf_op jit(solution)/shard_map/all_gather | solution.py:57
  54.7 309.8 %all-gather.5.cloned.1.call-start = ((), (), s32[]{:S(2)}) async-start(), calls=%async_computation.3 | async-start | bytes 4456448 | tf_op jit(solution)/shard_map/all_gather | solution.py:61
  364.5 3.0 copy-start.1
  367.5 3.0 copy-start.2
  367.5 3.1 copy-start.3
Sparse Core Ops, SparseCore 0:
  54.8 209.3 all-gather.2
  266.3 98.1 all-gather.4
where the time goes:
time: 432 us
  waiting for transfers between devices  323 us (75%)
  blocking collectives  51.9 us (12%)
  starting transfers between devices  16.2 us (4%)
  between operations  13.5 us (3%)
  local copies, waits for them, and re-layouts  11.6 us (3%)
  matrix products  11.5 us (3%)
    all_gather x1, waiting for transfers between devices, on_device(): residual_rows = lax.all_gather(residual_piece, 'src', axis=1, tiled=True)  209 us
    all_gather x1, waiting for transfers between devices, on_device(): piece = lax.all_gather(green_fields, 'slab', axis=1, tiled=True)  89.8 us
    psum x1, blocking collectives, on_device(): return lax.psum(partial_value, 'slab')  51.9 us
    all_to_all x1, waiting for transfers between devices, on_device(): lax.all_to_all(sent_values.reshape(slab_count, capacity, width), 'slab',...  14.7 us
    all_to_all x1, starting transfers between devices, on_device(): lax.all_to_all(sent_labels.reshape(slab_count, capacity, 2), 'slab', spli...  12.6 us
    all_to_all x1, waiting for transfers between devices, on_device(): lax.all_to_all(sent_labels.reshape(slab_count, capacity, 2), 'slab', spli...  9.19 us
  transfers between devices with their start and end apart: 4, of which 4 were waited for; matrix products, arithmetic and copies ran while one was open for 3% of the time, Pallas kernels for 0%

commit v1 on v0

--- a/solution.py
+++ b/solution.py
@@ -54,7 +54,8 @@
     ).astype(jnp.bfloat16)
     assembled = jnp.dot(picks, got_values.reshape(-1, width), preferred_element_type=jnp.float32)
     residual_piece = assembled.astype(jnp.bfloat16)
-    residual_rows = lax.all_gather(residual_piece, "src", axis=1, tiled=True)
+    tiles = lax.all_gather(residual_piece, "src")
+    residual_rows = jnp.concatenate(tiles, axis=1)
     split_rows = residual_rows.reshape(sources_here, src_count, 2, half_width)
     res_real = split_rows[:, :, 0, :].reshape(sources_here, src_count * half_width)
     res_imag = split_rows[:, :, 1, :].reshape(sources_here, src_count * half_width)

time: 432 us -> 391 us (0.905)
  waiting for transfers between devices: 323 us -> 282 us
    all_gather x1, waiting for transfers between devices: 209 us -> 160 us  [on_device(): tiles = lax.all_gather(residual_piece, 'src')]
    all_gather x1, waiting for transfers between devices: 89.8 us -> 97.1 us  [on_device(): piece = lax.all_gather(green_fields, 'slab', axis=1, tiled=True)]
where the time goes in v1:
time: 391 us
  waiting for transfers between devices  282 us (72%)
  blocking collectives  51.9 us (13%)
  starting transfers between devices  16.2 us (4%)
  between operations  13.5 us (3%)
  local copies, waits for them, and re-layouts  11.6 us (3%)
  matrix products  11.5 us (3%)
  other arithmetic  4.07 us (1%)
    all_gather x1, waiting for transfers between devices, on_device(): tiles = lax.all_gather(residual_piece, 'src')  160 us
    all_gather x1, waiting for transfers between devices, on_device(): piece = lax.all_gather(green_fields, 'slab', axis=1, tiled=True)  97.1 us
    psum x1, blocking collectives, on_device(): return lax.psum(partial_value, 'slab')  51.9 us
    all_to_all x1, waiting for transfers between devices, on_device(): lax.all_to_all(sent_values.reshape(slab_count, capacity, width), 'slab',...  14.7 us
    all_to_all x1, starting transfers between devices, on_device(): lax.all_to_all(sent_labels.reshape(slab_count, capacity, 2), 'slab', spli...  12.6 us
    all_to_all x1, waiting for transfers between devices, on_device(): lax.all_to_all(sent_labels.reshape(slab_count, capacity, 2), 'slab', spli...  9.19 us
  transfers between devices with their start and end apart: 4, of which 4 were waited for; matrix products, arithmetic and copies ran while one was open for 3% of the time, Pallas kernels for 0%

profile of v1, /device:TPU:6, one launch (start us, length us, event | category | flops | bytes accessed | tf_op | source)
XLA Modules:
  0.0 391.0 jit_solution(7246964289313251789)
XLA Ops:
  6.5 0.7 fusion.31
  7.3 1.1 reduce-window.6
  8.4 0.2 slice_reduce_fusion
  8.7 0.8 fusion.30
  9.4 0.7 add_add_fusion
  10.1 0.7 add_convert_fusion
  10.8 0.5 fusion.21
  11.4 0.6 copy.12
  12.0 12.6 %all-to-all-start = ((bf16[16,64,2]{1,2,0:T(2,128)(2,1)}), bf16[16,64,2]{1,2,0:T(2,128)(2,1)S(1)}, u32[]{:S(2)}, u32[]{:S(2)}) async-start(bf16[16,64,2]{1,2,0:T(2,128)(2,1)} %copy.12), calls=%async_computation | async-start | bytes 16384 | tf_op jit(solution)/shard_map/all_to_all | solution.py:42
  24.6 1.2 fusion.16
  25.8 9.2 %all-to-all-done = bf16[16,64,2]{1,2,0:T(2,128)(2,1)S(1)} async-done(((bf16[16,64,2]{1,2,0:T(2,128)(2,1)}), bf16[16,64,2]{1,2,0:T(2,128)(2,1)S(1)}, u32[]{:S(2)}, u32[]{:S(2)}) %all-to-all-start) | async-done | bytes 4128 | tf_op jit(solution)/shard_map/all_to_all | solution.py:42
  35.0 3.5 all-to-all-start.1
  38.7 14.7 %all-to-all-done.1 = bf16[16,64,128]{2,1,0:T(8,128)(2,1)S(1)} async-done(((bf16[16,64,128]{2,1,0:T(8,128)(2,1)}), bf16[16,64,128]{2,1,0:T(8,128)(2,1)S(1)}, u32[]{:S(2)}, u32[]{:S(2)}) %all-to-all-start.1) | async-done | bytes 262176 | tf_op jit(solution)/shard_map/all_to_all | solution.py:35
  53.4 1.3 fusion.17
  54.8 0.7 all-gather.4.cloned.1.call-update
  55.5 160.5 %all-gather.6.cloned.1.call-done = bf16[16384,128]{1,0:T(8,128)(2,1)} async-done(((bf16[512,128]{1,0:T(8,128)(2,1)}), bf16[16384,128]{1,0:T(8,128)(2,1)}) %all-gather.6.cloned.1.call-update) | async-done | bytes 4194320 | tf_op jit(solution)/shard_map/all_gather | solution.py:57
  215.9 6.5 %copy.14 = bf16[32,512,128]{1,2,0:T(8,128)(2,1)} copy(bf16[32,512,128]{2,1,0:T(8,128)(2,1)} %bitcast.82) | data formatting | bytes 8388608 | tf_op jit(solution)/shard_map/all_gather | solution.py:57
  222.5 4.0 %fusion.47 = (bf16[512,32,1,64]{0,3,2,1:T(8,128)(2,1)}, bf16[512,32,1,64]{0,3,2,1:T(8,128)(2,1)S(1)}) fusion(bf16[512,32,2,64]{0,3,2,1:T(8,128)(2,1)} %bitcast.81), kind=kLoop, calls=%fused_computation.67 | loop fusion | bytes 8388608 | tf_op jit(solution)/shard_map/slice | solution.py:61
  226.4 97.1 %all-gather.4.cloned.1.call-done = bf16[2,2048,512]{2,1,0:T(8,128)(2,1)} async-done(((bf16[2,128,512]{2,1,0:T(8,128)(2,1)}), bf16[2,2048,512]{2,1,0:T(8,128)(2,1)}) %all-gather.4.cloned.1.call-update) | async-done | bytes 4194320 | tf_op jit(solution)/shard_map/all_gather | solution.py:62
  323.5 3.0 fusion.7
  326.5 3.0 fusion.6
  329.6 1.3 fusion.11
  330.9 1.3 fusion.15
  332.2 51.9 %psum.7 = f32[512]{0:T(512)} all-reduce(f32[512]{0:T(512)S(1)} %fusion.15), channel_id=1, replica_groups=mesh['slab'=16,'src'=32] {'slab'}, use_global_device_ids=true, to_apply=%region_4.5 | all-reduce | flops 512 | bytes 4096 | tf_op jit(solution)/shard_map/psum | solution.py:75
  (19 shorter events, 0.4 us)
Async XLA Ops:
  6.5 18.1 %copy-start = (bf16[1,512,128]{2,1,0:T(8,128)(2,1)S(1)}, bf16[1,512,128]{2,1,0:T(8,128)(2,1)}, u32[]{:S(2)}) copy-start(bf16[1,512,128]{2,1,0:T(8,128)(2,1)} %param.5) | copy-start | bytes 393220
  12.0 23.0 %all-to-all-start = ((bf16[16,64,2]{1,2,0:T(2,128)(2,1)}), bf16[16,64,2]{1,2,0:T(2,128)(2,1)S(1)}, u32[]{:S(2)}, u32[]{:S(2)}) async-start(bf16[16,64,2]{1,2,0:T(2,128)(2,1)} %copy.12), calls=%async_computation | async-start | bytes 16384 | tf_op jit(solution)/shard_map/all_to_all | solution.py:42
  35.0 18.5 %all-to-all-start.1 = ((bf16[16,64,128]{2,1,0:T(8,128)(2,1)}), bf16[16,64,128]{2,1,0:T(8,128)(2,1)S(1)}, u32[]{:S(2)}, u32[]{:S(2)}) async-start(bf16[16,64,128]{2,1,0:T(8,128)(2,1)} %bitcast.6), calls=%async_computation.1 | async-start | bytes 524288 | tf_op jit(solution)/shard_map/all_to_all | solution.py:35
  38.5 177.4 %all-gather.6.cloned.1.call-start = ((), (), s32[]{:S(2)}) async-start(), calls=%async_computation.3 | async-start | bytes 4325376 | tf_op jit(solution)/shard_map/all_gather | solution.py:57
  54.7 268.8 %all-gather.4.cloned.1.call-start = ((), (), s32[]{:S(2)}) async-start(), calls=%async_computation.2 | async-start | bytes 4456448 | tf_op jit(solution)/shard_map/all_gather | solution.py:62
  323.5 3.0 copy-start.1
  326.5 3.1 copy-start.2
  326.5 3.1 copy-start.3
Sparse Core Ops, SparseCore 0:
  54.8 161.0 all-gather.5
  218.0 105.4 all-gather.3
